TPU v7x, 256 devices: a whole 4x4x8 slice. The times are simulated.
256 devices in a mesh: layer: 4 (over y), front: 64 (over z, x, core).
Axes of the slice: x: 4, y: 4, z: 8, core: 2. Of those that a mesh axis runs over, the one named last changes fastest.
Arguments:
- right_sides: float32 [4, 2, 4, 8192], P('layer', None, None, 'front'), may hold values from -6 to 6
- leaf_inverse: bfloat16 [4, 2, 8192, 128], P('layer', None, 'front'), may hold values from -0.375 to 0.375
- couple_above: bfloat16 [4, 2, 8192, 128], P('layer', None, 'front'), may hold values from -0.1875 to 0.1875
- couple_below: bfloat16 [4, 2, 8192, 128], P('layer', None, 'front'), may hold values from -0.1875 to 0.1875
- sep_gather: bfloat16 [4, 2, 5120, 8192], P('layer', None, None, 'front'), may hold values from -0.046875 to 0.046875
- sep_inverse: bfloat16 [4, 2, 5120, 5120], P('layer', None, 'front'), may hold values from -0.0625 to 0.0625
- sep_spread: bfloat16 [4, 2, 8192, 5120], P('layer', None, 'front'), may hold values from -0.0625 to 0.0625
- panel_owner: int32 [4, 64], P('layer'), may hold values from 0 to 63, each once within a row
Outputs:
- solution: float32 [4, 2, 4, 8192], P('layer', None, None, 'front')
Inputs may be any that keep to these rules, and one draw needn't show every extreme that they name: Each row of panel_owner names every slot 0 to 63 once.
All inputs are finite; a program needn't handle non-finite values.
Results may differ from a plain program's by a relative error of at most 0.023.
Values may be sent and summed in bfloat16 or wider, within the bound.
A program may use at most 128 MiB of HBM per device.

v0:
```python
import jax
import jax.numpy as jnp
from jax import lax
from jax.sharding import PartitionSpec as P


def from_behind(block, axis, distance):
    devices = range(lax.axis_size(axis))
    route = [(i - distance, i) for i in devices if i - distance in devices]
    return lax.ppermute(block, axis, route)


def dense_apply(matrix, vector):

    def single(left, right):
        return jnp.dot(right, left.T, preferred_element_type=jnp.float32)

    real_part = single(matrix[0], vector[0]) - single(matrix[1], vector[1])
    imag_part = single(matrix[0], vector[1]) + single(matrix[1], vector[0])
    return jnp.stack([real_part, imag_part])


def layer_solve(source, leaf, gather_map, sep_panel, spread, owner_row):
    leaf_values = dense_apply(leaf, source.astype(jnp.bfloat16))
    partial_sums = dense_apply(gather_map, leaf_values.astype(jnp.bfloat16))
    sep_rounded = lax.psum(partial_sums, "front").astype(jnp.bfloat16)
    own_rows = dense_apply(sep_panel, sep_rounded).astype(jnp.bfloat16)
    stored = lax.all_gather(own_rows, "front", axis=2, tiled=True)
    count = stored.shape[1]
    panels = stored.reshape(2, count, owner_row.shape[0], own_rows.shape[2])
    sep_values = jnp.take(panels, owner_row, axis=2).reshape(2, count, stored.shape[2])
    return leaf_values - dense_apply(spread, sep_values)


def local(
    right_sides,
    leaf_inverse,
    couple_above,
    couple_below,
    sep_gather,
    sep_inverse,
    sep_spread,
    panel_owner,
):
    depth = lax.axis_size("layer")
    owner_row = panel_owner[0]
    sources = right_sides[0]

    def solve(source):
        return layer_solve(
            source, leaf_inverse[0], sep_gather[0], sep_inverse[0], sep_spread[0], owner_row
        )

    forward = solve(sources)
    for step_index in range(depth - 1):
        from_prev = from_behind(forward.astype(jnp.bfloat16), "layer", 1)
        forward = solve(sources - dense_apply(couple_above[0], from_prev))
    solution = forward
    for step_index in range(depth - 1):
        from_next = from_behind(solution.astype(jnp.bfloat16), "layer", -1)
        solution = forward - solve(dense_apply(couple_below[0], from_next))
    return solution[None]


def solution(mesh):
    return jax.shard_map(
        local,
        mesh=mesh,
        in_specs=(
            P("layer", None, None, "front"),
            P("layer", None, "front", None),
            P("layer", None, "front", None),
            P("layer", None, "front", None),
            P("layer", None, None, "front"),
            P("layer", None, "front", None),
            P("layer", None, "front", None),
            P("layer", None),
        ),
        out_specs=P("layer", None, None, "front"),
        check_vma=False,
    )
```

profile of v0, /device:TPU:1, one launch (start us, length us, event | category | flops | bytes accessed | tf_op | source)
XLA Modules:
  0.0 2287.0 jit_solution(15067838010511855414)
XLA Ops:
  10.3 249.5 %all-reduce.7 = bf16[2,4,5120]{2,1,0:T(4,128)(2,1)S(1)} all-reduce(f32[2,4,5120]{2,1,0:T(4,128)S(1)} %pad_maximum_fusion), channel_id=1, replica_groups=mesh['layer'=4,'front'=64] {'front'}, use_global_device_ids=true, to_apply=%region_0.0 | all-reduce | flops 40960 | bytes 245760 | tf_op jit(solution)/shard_map/psum | solution.py:26
  263.7 58.7 %all_gather.21 = bf16[2,4,5120]{1,0,2:T(2,128)(2,1)} all-gather(bf16[2,4,80]{1,0,2:T(2,128)(2,1)S(1)} %copy.58), channel_id=1, replica_groups=mesh['layer'=4,'front'=64] {'front'}, dimensions={2}, use_global_device_ids=true | all-gather | bytes 83200 | tf_op jit(solution)/shard_map/all_gather | solution.py:28
  322.4 5.4 copy.60
  333.7 3.2 collective-permute-start
  340.8 243.3 %all-reduce.8 = bf16[2,4,5120]{2,1,0:T(4,128)(2,1)S(1)} all-reduce(f32[2,4,5120]{2,1,0:T(4,128)S(1)} %pad_maximum_fusion.1), channel_id=1, replica_groups=mesh['layer'=4,'front'=64] {'front'}, use_global_device_ids=true, to_apply=%region_1.0 | all-reduce | flops 40960 | bytes 245760 | tf_op jit(solution)/shard_map/psum | solution.py:26
  588.0 59.3 %all_gather.22 = bf16[2,4,5120]{1,0,2:T(2,128)(2,1)} all-gather(bf16[2,4,80]{1,0,2:T(2,128)(2,1)S(1)} %copy.63), channel_id=1, replica_groups=mesh['layer'=4,'front'=64] {'front'}, dimensions={2}, use_global_device_ids=true | all-gather | bytes 83200 | tf_op jit(solution)/shard_map/all_gather | solution.py:28
  647.2 5.4 copy.65
  655.7 1.9 fusion.34
  659.8 3.6 collective-permute-start.1
  667.2 243.3 %all-reduce.9 = bf16[2,4,5120]{2,1,0:T(4,128)(2,1)S(1)} all-reduce(f32[2,4,5120]{2,1,0:T(4,128)S(1)} %pad_maximum_fusion.2), channel_id=1, replica_groups=mesh['layer'=4,'front'=64] {'front'}, use_global_device_ids=true, to_apply=%region_2.4 | all-reduce | flops 40960 | bytes 245760 | tf_op jit(solution)/shard_map/psum | solution.py:26
  914.4 58.7 %all_gather.23 = bf16[2,4,5120]{1,0,2:T(2,128)(2,1)} all-gather(bf16[2,4,80]{1,0,2:T(2,128)(2,1)S(1)} %copy.68), channel_id=1, replica_groups=mesh['layer'=4,'front'=64] {'front'}, dimensions={2}, use_global_device_ids=true | all-gather | bytes 83200 | tf_op jit(solution)/shard_map/all_gather | solution.py:28
  973.1 5.4 copy.70
  981.6 1.9 fusion.30
  985.7 3.6 collective-permute-start.2
  993.1 243.5 %all-reduce.10 = bf16[2,4,5120]{2,1,0:T(4,128)(2,1)S(1)} all-reduce(f32[2,4,5120]{2,1,0:T(4,128)S(1)} %pad_maximum_fusion.3), channel_id=1, replica_groups=mesh['layer'=4,'front'=64] {'front'}, use_global_device_ids=true, to_apply=%region_3.5 | all-reduce | flops 40960 | bytes 245760 | tf_op jit(solution)/shard_map/psum | solution.py:26
  1240.5 58.7 %all_gather.24 = bf16[2,4,5120]{1,0,2:T(2,128)(2,1)} all-gather(bf16[2,4,80]{1,0,2:T(2,128)(2,1)S(1)} %copy.73), channel_id=1, replica_groups=mesh['layer'=4,'front'=64] {'front'}, dimensions={2}, use_global_device_ids=true | all-gather | bytes 83200 | tf_op jit(solution)/shard_map/all_gather | solution.py:28
  1299.2 5.4 copy.75
  1307.7 1.9 fusion.26
  1313.2 3.3 collective-permute-done.3
  1319.5 243.3 %all-reduce.11 = bf16[2,4,5120]{2,1,0:T(4,128)(2,1)S(1)} all-reduce(f32[2,4,5120]{2,1,0:T(4,128)S(1)} %pad_maximum_fusion.4), channel_id=1, replica_groups=mesh['layer'=4,'front'=64] {'front'}, use_global_device_ids=true, to_apply=%region_4.6 | all-reduce | flops 40960 | bytes 245760 | tf_op jit(solution)/shard_map/psum | solution.py:26
  1566.7 58.7 %all_gather.25 = bf16[2,4,5120]{1,0,2:T(2,128)(2,1)} all-gather(bf16[2,4,80]{1,0,2:T(2,128)(2,1)S(1)} %copy.78), channel_id=1, replica_groups=mesh['layer'=4,'front'=64] {'front'}, dimensions={2}, use_global_device_ids=true | all-gather | bytes 83200 | tf_op jit(solution)/shard_map/all_gather | solution.py:28
  1625.4 5.4 copy.80
  1633.9 1.9 fusion.22
  1639.6 2.8 collective-permute-done.4
  1645.4 243.3 %all-reduce.12 = bf16[2,4,5120]{2,1,0:T(4,128)(2,1)S(1)} all-reduce(f32[2,4,5120]{2,1,0:T(4,128)S(1)} %pad_maximum_fusion.5), channel_id=1, replica_groups=mesh['layer'=4,'front'=64] {'front'}, use_global_device_ids=true, to_apply=%region_5.7 | all-reduce | flops 40960 | bytes 245760 | tf_op jit(solution)/shard_map/psum | solution.py:26
  1892.6 58.7 %all_gather.26 = bf16[2,4,5120]{1,0,2:T(2,128)(2,1)} all-gather(bf16[2,4,80]{1,0,2:T(2,128)(2,1)S(1)} %copy.83), channel_id=1, replica_groups=mesh['layer'=4,'front'=64] {'front'}, dimensions={2}, use_global_device_ids=true | all-gather | bytes 83200 | tf_op jit(solution)/shard_map/all_gather | solution.py:28
  1951.3 5.4 copy.85
  1959.8 1.9 fusion.18
  1965.3 3.0 collective-permute-done.5
  1971.3 243.4 %all-reduce.13 = bf16[2,4,5120]{2,1,0:T(4,128)(2,1)S(1)} all-reduce(f32[2,4,5120]{2,1,0:T(4,128)S(1)} %pad_maximum_fusion.6), channel_id=1, replica_groups=mesh['layer'=4,'front'=64] {'front'}, use_global_device_ids=true, to_apply=%region_6.8 | all-reduce | flops 40960 | bytes 245760 | tf_op jit(solution)/shard_map/psum | solution.py:26
  2218.5 59.0 %all_gather.27 = bf16[2,4,5120]{1,0,2:T(2,128)(2,1)} all-gather(bf16[2,4,80]{1,0,2:T(2,128)(2,1)S(1)} %copy.88), channel_id=1, replica_groups=mesh['layer'=4,'front'=64] {'front'}, dimensions={2}, use_global_device_ids=true | all-gather | bytes 83200 | tf_op jit(solution)/shard_map/all_gather | solution.py:28
  2277.5 5.5 copy.90
  (265 shorter events, 97.6 us)
Async XLA Ops:
  0.0 9.3 copy-start
  259.8 3.1 copy-start.12
  329.1 3.7 copy-start.1
  332.8 4.9 copy-start.9
  332.8 5.4 copy-start.11
  332.8 5.5 copy-start.8
  333.7 3.9 collective-permute-start
  584.1 3.1 copy-start.13
  655.6 3.7 copy-start.2
  659.8 4.3 collective-permute-start.1
  910.5 3.1 copy-start.14
  981.6 3.7 copy-start.3
  985.7 4.3 collective-permute-start.2
  1236.6 3.1 copy-start.15
  1307.7 3.7 copy-start.4
  1309.6 6.9 copy-start.10
  1311.9 4.6 collective-permute-start.3
  1562.8 3.1 copy-start.16
  1633.9 3.7 copy-start.5
  1638.0 4.3 collective-permute-start.4
  1888.7 3.1 copy-start.17
  1959.8 3.7 copy-start.6
  1964.0 4.3 collective-permute-start.5
  1971.3 246.4 %copy-start.18 = (bf16[1,2,80,5120]{3,2,1,0:T(8,128)(2,1)S(1)}, bf16[1,2,80,5120]{3,2,1,0:T(8,128)(2,1)}, u32[]{:S(2)}) copy-start(bf16[1,2,80,5120]{3,2,1,0:T(8,128)(2,1)} %param.15) | copy-start | bytes 4915204
  2277.5 6.7 copy-start.7
where the time goes:
time: 2300 us; the launch traced here: 2290 us
  blocking collectives  2120 us (92%)
  matrix products  87.5 us (4%)
  local copies, waits for them, and re-layouts  46.7 us (2%)
    psum x7, blocking collectives, layer_solve(): sep_rounded = lax.psum(partial_sums, 'front').astype(jnp.bfloat16)  1710 us
    all_gather x7, blocking collectives, layer_solve(): stored = lax.all_gather(own_rows, 'front', axis=2, tiled=True)  412 us
    dot_general x136, matrix products, single(): return jnp.dot(right, left.T, preferred_element_type=jnp.float32)  87.5 us
  transfers between devices with their start and end apart: 6, of which 6 were waited for; matrix products, arithmetic and copies ran while one was open for 0% of the time, Pallas kernels for 0%

commit v1 on v0

--- a/solution.py
+++ b/solution.py
@@ -25,7 +25,9 @@
     partial_sums = dense_apply(gather_map, leaf_values.astype(jnp.bfloat16))
     sep_rounded = lax.psum(partial_sums, "front").astype(jnp.bfloat16)
     own_rows = dense_apply(sep_panel, sep_rounded).astype(jnp.bfloat16)
-    stored = lax.all_gather(own_rows, "front", axis=2, tiled=True)
+    stored = jnp.concatenate(
+        lax.all_to_all(jnp.stack([own_rows] * lax.axis_size("front")), "front", 0, 0), axis=2
+    )
     count = stored.shape[1]
     panels = stored.reshape(2, count, owner_row.shape[0], own_rows.shape[2])
     sep_values = jnp.take(panels, owner_row, axis=2).reshape(2, count, stored.shape[2])

time: 2300 us -> 1980 us (0.86)
  blocking collectives: 2120 us -> 1830 us
  local copies, waits for them, and re-layouts: 46.7 us -> 9.15 us
    all_gather x7 -> x0, blocking collectives: 412 us -> none  [layer_solve(): stored = lax.all_gather(own_rows, 'front', axis=2, tiled=True)]
    all_to_all x0 -> x6, blocking collectives: none -> 125 us  [layer_solve(): lax.all_to_all(jnp.stack([own_rows] * lax.axis_size('front')), 'front', 0...]
    reshape x7 -> x0, local copies, waits for them, and re-layouts: 37.8 us -> none  [layer_solve(): panels = stored.reshape(2, count, owner_row.shape[0], own_rows.shape[2])]
  transfers between devices with their start and end apart: 6 -> 7, of which waited for: 6 -> 7; matrix products, arithmetic and copies ran while one was open for 0% -> 0% of each run, Pallas kernels for 0% -> 0%
where the time goes in v1:
time: 1980 us
  blocking collectives  1830 us (92%)
  matrix products  90 us (5%)
  starting transfers between devices  24.2 us (1%)
  waiting for transfers between devices  22.6 us (1%)
    psum x7, blocking collectives, layer_solve(): sep_rounded = lax.psum(partial_sums, 'front').astype(jnp.bfloat16)  1700 us
    all_to_all x6, blocking collectives, layer_solve(): lax.all_to_all(jnp.stack([own_rows] * lax.axis_size('front')), 'front', 0...  125 us
    dot_general x136, matrix products, single(): return jnp.dot(right, left.T, preferred_element_type=jnp.float32)  90 us
  transfers between devices with their start and end apart: 7, of which 7 were waited for; matrix products, arithmetic and copies ran while one was open for 0% of the time, Pallas kernels for 0%

profile of v1, /device:TPU:1, one launch (start us, length us, event | category | flops | bytes accessed | tf_op | source)
XLA Modules:
  0.0 1976.5 jit_solution(1031925313824171566)
XLA Ops:
  4.5 1.8 fusion.108
  9.0 249.5 %all-reduce.7 = bf16[2,4,5120]{2,1,0:T(4,128)(2,1)S(1)} all-reduce(f32[2,4,5120]{2,1,0:T(4,128)S(1)} %pad_maximum_fusion), channel_id=1, replica_groups=mesh['layer'=4,'front'=64] {'front'}, use_global_device_ids=true, to_apply=%region_0.0 | all-reduce | flops 40960 | bytes 245760 | tf_op jit(solution)/shard_map/psum | solution.py:26
  263.0 9.7 all-to-all-start
  272.7 11.3 all-to-all-done
  285.4 1.9 fusion.40
  290.0 3.2 collective-permute-start
  297.0 241.9 %all-reduce.8 = bf16[2,4,5120]{2,1,0:T(4,128)(2,1)S(1)} all-reduce(f32[2,4,5120]{2,1,0:T(4,128)S(1)} %pad_maximum_fusion.1), channel_id=1, replica_groups=mesh['layer'=4,'front'=64] {'front'}, use_global_device_ids=true, to_apply=%region_1.0 | all-reduce | flops 40960 | bytes 245760 | tf_op jit(solution)/shard_map/psum | solution.py:26
  542.7 20.8 %all_to_all.35 = bf16[64,2,4,80]{3,2,1,0:T(4,128)(2,1)S(1)} all-to-all(bf16[64,2,4,80]{3,2,1,0:T(4,128)(2,1)S(1)} %stack.249), channel_id=1, replica_groups=mesh['layer'=4,'front'=64] {'front'}, dimensions={0} | all-to-all | bytes 163840 | tf_op jit(solution)/shard_map/all_to_all | solution.py:29
  566.5 1.9 fusion.34
  568.4 1.8 fusion.127
  570.7 3.6 collective-permute-start.1
  578.1 242.0 %all-reduce.9 = bf16[2,4,5120]{2,1,0:T(4,128)(2,1)S(1)} all-reduce(f32[2,4,5120]{2,1,0:T(4,128)S(1)} %pad_maximum_fusion.2), channel_id=1, replica_groups=mesh['layer'=4,'front'=64] {'front'}, use_global_device_ids=true, to_apply=%region_2.4 | all-reduce | flops 40960 | bytes 245760 | tf_op jit(solution)/shard_map/psum | solution.py:26
  823.9 20.9 %all_to_all.36 = bf16[64,2,4,80]{3,2,1,0:T(4,128)(2,1)S(1)} all-to-all(bf16[64,2,4,80]{3,2,1,0:T(4,128)(2,1)S(1)} %stack.265), channel_id=1, replica_groups=mesh['layer'=4,'front'=64] {'front'}, dimensions={0} | all-to-all | bytes 163840 | tf_op jit(solution)/shard_map/all_to_all | solution.py:29
  847.9 1.9 fusion.30
  849.8 1.8 fusion.139
  852.0 3.6 collective-permute-start.2
  859.5 242.0 %all-reduce.10 = bf16[2,4,5120]{2,1,0:T(4,128)(2,1)S(1)} all-reduce(f32[2,4,5120]{2,1,0:T(4,128)S(1)} %pad_maximum_fusion.3), channel_id=1, replica_groups=mesh['layer'=4,'front'=64] {'front'}, use_global_device_ids=true, to_apply=%region_3.5 | all-reduce | flops 40960 | bytes 245760 | tf_op jit(solution)/shard_map/psum | solution.py:26
  1105.2 20.9 %all_to_all.37 = bf16[64,2,4,80]{3,2,1,0:T(4,128)(2,1)S(1)} all-to-all(bf16[64,2,4,80]{3,2,1,0:T(4,128)(2,1)S(1)} %stack.284), channel_id=1, replica_groups=mesh['layer'=4,'front'=64] {'front'}, dimensions={0} | all-to-all | bytes 163840 | tf_op jit(solution)/shard_map/all_to_all | solution.py:29
  1129.3 1.9 fusion.26
  1131.2 1.8 fusion.148
  1134.7 3.3 collective-permute-done.3
  1141.1 242.0 %all-reduce.11 = bf16[2,4,5120]{2,1,0:T(4,128)(2,1)S(1)} all-reduce(f32[2,4,5120]{2,1,0:T(4,128)S(1)} %pad_maximum_fusion.4), channel_id=1, replica_groups=mesh['layer'=4,'front'=64] {'front'}, use_global_device_ids=true, to_apply=%region_4.6 | all-reduce | flops 40960 | bytes 245760 | tf_op jit(solution)/shard_map/psum | solution.py:26
  1386.9 20.9 %all_to_all.38 = bf16[64,2,4,80]{3,2,1,0:T(4,128)(2,1)S(1)} all-to-all(bf16[64,2,4,80]{3,2,1,0:T(4,128)(2,1)S(1)} %stack.300), channel_id=1, replica_groups=mesh['layer'=4,'front'=64] {'front'}, dimensions={0} | all-to-all | bytes 163840 | tf_op jit(solution)/shard_map/all_to_all | solution.py:29
  1410.9 1.9 fusion.22
  1416.6 2.8 collective-permute-done.4
  1422.4 242.1 %all-reduce.12 = bf16[2,4,5120]{2,1,0:T(4,128)(2,1)S(1)} all-reduce(f32[2,4,5120]{2,1,0:T(4,128)S(1)} %pad_maximum_fusion.5), channel_id=1, replica_groups=mesh['layer'=4,'front'=64] {'front'}, use_global_device_ids=true, to_apply=%region_5.7 | all-reduce | flops 40960 | bytes 245760 | tf_op jit(solution)/shard_map/psum | solution.py:26
  1668.4 20.8 %all_to_all.39 = bf16[64,2,4,80]{3,2,1,0:T(4,128)(2,1)S(1)} all-to-all(bf16[64,2,4,80]{3,2,1,0:T(4,128)(2,1)S(1)} %stack.313), channel_id=1, replica_groups=mesh['layer'=4,'front'=64] {'front'}, dimensions={0} | all-to-all | bytes 163840 | tf_op jit(solution)/shard_map/all_to_all | solution.py:29
  1692.2 1.9 fusion.18
  1694.1 1.8 fusion.169
  1697.7 3.0 collective-permute-done.5
  1703.8 242.1 %all-reduce.13 = bf16[2,4,5120]{2,1,0:T(4,128)(2,1)S(1)} all-reduce(f32[2,4,5120]{2,1,0:T(4,128)S(1)} %pad_maximum_fusion.6), channel_id=1, replica_groups=mesh['layer'=4,'front'=64] {'front'}, use_global_device_ids=true, to_apply=%region_6.8 | all-reduce | flops 40960 | bytes 245760 | tf_op jit(solution)/shard_map/psum | solution.py:26
  1952.0 20.8 %all_to_all.40 = bf16[64,2,4,80]{3,2,1,0:T(4,128)(2,1)S(1)} all-to-all(bf16[64,2,4,80]{3,2,1,0:T(4,128)(2,1)S(1)} %stack.326), channel_id=1, replica_groups=mesh['layer'=4,'front'=64] {'front'}, dimensions={0} | all-to-all | bytes 163840 | tf_op jit(solution)/shard_map/all_to_all | solution.py:29
  (266 shorter events, 88.3 us)
Async XLA Ops:
  0.0 8.0 copy-start
  258.5 3.1 copy-start.12
  260.1 12.6 copy-start.18
  263.0 21.0 %all-to-all-start = ((bf16[64,2,4,80]{3,2,1,0:T(4,128)(2,1)}), bf16[64,2,4,80]{3,2,1,0:T(4,128)(2,1)S(1)}, u32[]{:S(2)}, u32[]{:S(2)}) async-start(bf16[64,2,4,80]{3,2,1,0:T(4,128)(2,1)} %stack.233), calls=%async_computation | async-start | bytes 262144 | tf_op jit(solution)/shard_map/all_to_all | solution.py:29
  285.3 3.7 copy-start.1
  289.0 4.9 copy-start.9
  289.0 5.4 copy-start.11
  289.0 5.5 copy-start.8
  290.0 3.9 collective-permute-start
  538.9 3.1 copy-start.13
  566.5 3.7 copy-start.2
  570.7 4.3 collective-permute-start.1
  820.1 3.1 copy-start.14
  847.9 3.7 copy-start.3
  852.0 4.3 collective-permute-start.2
  1101.4 3.1 copy-start.15
  1129.2 3.7 copy-start.4
  1131.2 6.9 copy-start.10
  1133.4 4.6 collective-permute-start.3
  1383.1 3.1 copy-start.16
  1410.9 3.7 copy-start.5
  1415.0 4.3 collective-permute-start.4
  1664.6 3.1 copy-start.17
  1692.2 3.7 copy-start.6
  1696.4 4.3 collective-permute-start.5
  1948.8 25.1 %copy-start.7 = (bf16[1,2,128,5120]{3,2,1,0:T(8,128)(2,1)S(1)}, bf16[1,2,128,5120]{3,2,1,0:T(8,128)(2,1)}, u32[]{:S(2)}) copy-start(bf16[1,2,128,5120]{3,2,1,0:T(8,128)(2,1)} %param.16) | copy-start | bytes 7864324
